TPU v7x, 32 devices: a whole 2x2x4 slice. The times are simulated.
32 devices in a mesh: groups: 2 (over y), space: 4 (over z), freq: 2 (over x), band: 2 (over core).
Axes of the slice: x: 2, y: 2, z: 4, core: 2. Of those that a mesh axis runs over, the one named last changes fastest.
Arguments:
- snapshots: bfloat16 [16, 256, 32768], P(('freq', 'band'), None, ('groups', 'space')), parts along dimension 2, may hold values from -6 to 6
- weights: float32 [32768], P(('groups', 'space')), parts along dimension 0, may hold values from 0.25 to 2.5
- triads: int32 [64, 2], replicated, may hold values from 0 to 63, as said below
Outputs:
- bispectra: float32 [128, 512], P(('groups', 'space', 'freq', 'band')), parts along dimension 0
There are 2 independent parts, one for each index of `groups`. A program takes and returns all parts, laid end to end along the dimension named above; an argument that names none is the same for every part. Nothing has to cross between parts.
Inputs may be any that keep to these rules, and one draw needn't show every extreme that they name: `triads`: each row is a pair (k, l) with k >= l and k + l <= 63; all pairs are distinct; the pair (63, 0) is always present.
All inputs are finite; a program needn't handle non-finite values.
Results may differ from a plain program's by a relative error of at most 0.0078.
Values may be sent and summed in bfloat16 or wider, within the bound.
No kernel may reach another device: no remote copies, remote signals or barrier semaphores. Data moves between devices by JAX's collectives and lax.ppermute only.
A program may use at most 128 MiB of HBM per device.

v0:
```python
import math
import jax
import jax.numpy as jnp
from jax import lax
from jax.sharding import PartitionSpec as P

NB = 16
NF = 64


def make_table(length):
    time_steps = jnp.arange(length, dtype=jnp.int32)
    frequency = jnp.arange(NF, dtype=jnp.int32)
    phase_index = frequency[:, None] * time_steps[None, :] % length
    angle_grid = phase_index.astype(jnp.float32) * (2.0 * math.pi / length)
    hann_window = 0.5 - 0.5 * jnp.cos(time_steps.astype(jnp.float32) * (2.0 * math.pi / length))
    gain_factor = 1.0 / math.sqrt(3.0 * length / 8.0)
    cos_rows = hann_window[None, :] * jnp.cos(angle_grid) * gain_factor
    sin_rows = -hann_window[None, :] * jnp.sin(angle_grid) * gain_factor
    return jnp.concatenate([cos_rows, sin_rows], axis=0).astype(jnp.bfloat16)


def triad_block(spectra_grid, weights, triad_block_ids):
    first_freq = triad_block_ids[:, 0]
    second_freq = triad_block_ids[:, 1]
    third_freq = first_freq + second_freq
    first_spec = jnp.take(spectra_grid, first_freq, axis=2).astype(jnp.float32)
    second_spec = jnp.take(spectra_grid, second_freq, axis=2).astype(jnp.float32)
    third_spec = jnp.take(spectra_grid, third_freq, axis=2)
    prod_re = weights * (
        first_spec[:, 0] * second_spec[:, 0] - first_spec[:, 1] * second_spec[:, 1]
    )
    prod_im = weights * (
        first_spec[:, 0] * second_spec[:, 1] + first_spec[:, 1] * second_spec[:, 0]
    )
    field_a = jnp.stack([prod_re, prod_im], axis=1).astype(jnp.bfloat16)
    products = jnp.einsum(
        "ictx,jdtx->tcdij", field_a, third_spec, preferred_element_type=jnp.float32
    )
    real_part = products[:, 0, 0] + products[:, 1, 1]
    imag_part = products[:, 0, 1] - products[:, 1, 0]
    stacked = jnp.stack([real_part, imag_part], axis=1)
    return stacked.reshape(triad_block_ids.shape[0], 2 * NB * NB)


def block_terms(spectra, weights, triad_rows, point_scale):
    row_count = triad_rows.shape[0]
    columns = spectra.shape[2]
    spectra_grid = spectra.reshape(NB, 2, NF, columns)
    block_size = math.gcd(row_count, max(1, 32768 // columns))
    grouped = triad_rows.reshape(row_count // block_size, block_size, 2)

    def one_group(triad_block_ids):
        return triad_block(spectra_grid, weights, triad_block_ids) * point_scale

    result = lax.map(one_group, grouped)
    return result.reshape(row_count, 2 * NB * NB)


def per_device(snapshots, weights, triads):
    local_blocks, length, points = snapshots.shape
    dft_table = make_table(length)
    spec_local = jnp.einsum(
        "ct,btx->bcx", dft_table, snapshots, preferred_element_type=jnp.float32
    ).astype(jnp.bfloat16)
    point_scale = 1.0 / math.sqrt(points * lax.axis_size("space"))
    shard_count = lax.axis_size("freq") * lax.axis_size("band")
    spectra = lax.all_to_all(spec_local, ("freq", "band"), split_axis=2, concat_axis=0, tiled=True)
    own_points = points // shard_count
    weights_own = lax.dynamic_slice_in_dim(
        weights, lax.axis_index(("freq", "band")) * own_points, own_points
    )
    partial_sums = lax.psum_scatter(
        block_terms(spectra, weights_own, triads, point_scale),
        "space",
        scatter_dimension=0,
        tiled=True,
    )
    result = lax.psum_scatter(partial_sums, ("freq", "band"), scatter_dimension=0, tiled=True)
    return result


def solution(mesh):
    return jax.shard_map(
        per_device,
        mesh=mesh,
        in_specs=(P(("freq", "band"), None, ("groups", "space")), P(("groups", "space")), P()),
        out_specs=P(("groups", "space", "freq", "band"), None),
        check_vma=False,
    )
```

profile of v0, /device:TPU:0, one launch (start us, length us, event | category | flops | bytes accessed | tf_op | source)
XLA Modules:
  0.0 175.1 jit_solution(2965398846534315300)
XLA Ops:
  6.6 0.3 multiply_convert_fusion.2
  6.9 6.6 %fusion.11 = bf16[4,128,4096]{2,1,0:T(8,128)(2,1)} fusion(bf16[4,256,4096]{2,1,0:T(8,128)(2,1)} %param.7, bf16[64,256]{1,0:T(8,128)(2,1)S(1)} %get-tuple-element.80, bf16[64,256]{1,0:T(8,128)(2,1)S(1)} %get-tuple-element.81), kind=kOutput, calls=%fused_computation.35 | convolution fusion | flops 1075970048 | bytes 12648448 | tf_op jit(solution)/shard_map/ct,btx->bcx/dot_general | solution.py:63
  13.5 7.5 %copy.23 = bf16[4,128,4096]{1,0,2:T(4,128)(2,1)} copy(bf16[4,128,4096]{2,1,0:T(8,128)(2,1)} %fusion.11) | data formatting | bytes 8388608 | tf_op jit(solution)/shard_map/convert_element_type | solution.py:65
  21.1 0.0 copy-start.1
  21.1 5.0 %all-to-all-start = ((bf16[4,128,4096]{1,0,2:T(4,128)(2,1)}), bf16[4,128,4096]{1,0,2:T(4,128)(2,1)}, u32[]{:S(2)}, u32[]{:S(2)}) async-start(bf16[4,128,4096]{1,0,2:T(4,128)(2,1)} %copy.23), calls=%async_computation | async-start | bytes 8388608 | tf_op jit(solution)/shard_map/all_to_all | solution.py:68
  26.1 0.0 reduce-scatter.2.cloned.1.call-start
  26.1 0.0 copy-done.1
  26.1 0.1 reshape.77
  26.2 48.7 %all-to-all-done = bf16[4,128,4096]{1,0,2:T(4,128)(2,1)} async-done(((bf16[4,128,4096]{1,0,2:T(4,128)(2,1)}), bf16[4,128,4096]{1,0,2:T(4,128)(2,1)}, u32[]{:S(2)}, u32[]{:S(2)}) %all-to-all-start) | async-done | bytes 4194336 | tf_op jit(solution)/shard_map/all_to_all | solution.py:68
  74.9 10.0 %copy.24 = bf16[4,4,128,1024]{3,1,0,2:T(4,128)(2,1)} copy(bf16[4,4,128,1024]{2,1,3,0:T(4,128)(2,1)} %bitcast.17) | data formatting | bytes 8388608 | tf_op jit(solution)/shard_map/all_to_all | solution.py:68
  85.0 0.0 dynamic-slice-start
  85.0 6.9 %reshape.78 = bf16[16,2,64,1024]{3,0,2,1:T(8,128)(2,1)} reshape(bf16[4,4,128,1024]{3,1,0,2:T(4,128)(2,1)} %copy.24) | data formatting | bytes 8388608 | tf_op jit(solution)/shard_map/reshape | solution.py:49
  91.9 0.0 dynamic-slice-done
  91.9 0.0 copy-start.2
  91.9 43.5 %while.10 = (s32[]{:T(128)}, f32[2,32,512]{2,1,0:T(8,128)S(1)}, s32[2,32,2]{1,0,2:T(2,128)S(1)}, bf16[16,2,64,1024]{3,0,2,1:T(8,128)(2,1)}, f32[1024]{0:T(1024)S(1)}, /*index=5*/s32[]{:T(128)}) while((s32[]{:T(128)}, f32[2,32,512]{2,1,0:T(8,128)S(1)}, s32[2,32,2]{1,0,2:T(2,128)S(1)}, bf16[16,2,64,1024]{3,0,2,1:T(8,128)(2,1)}, ...), condition=%wide.region_1.3_spmd, body=%wide.region_0.2_spmd.sunk | while | flops 81841760 | bytes 40847500 | solution.py:56
  91.9 2.9 %gather_fusion.1 = bf16[32,16,2,1024]{3,1,2,0:T(8,128)(2,1)S(1)} fusion(bf16[16,2,64,1024]{3,0,2,1:T(8,128)(2,1)} %get-tuple-element.152, s32[1024]{0:T(1024)S(1)} %pad_clamp_fusion.7), kind=kCustom, calls=%fused_computation.1.clone.clone.1 | custom fusion | bytes 4194432 | tf_op jit(solution)/shard_map/while/body/eval_jaxpr/jit(_take)/gather | solution.py:27
  94.8 4.2 %gather_fusion = bf16[32,16,2,1024]{3,1,2,0:T(8,128)(2,1)} fusion(bf16[16,2,64,1024]{3,0,2,1:T(8,128)(2,1)} %get-tuple-element.152, s32[1024]{0:T(1024)S(1)} %pad_clamp_fusion.6), kind=kCustom, calls=%fused_computation.2.clone.clone.1 | custom fusion | bytes 4194432 | tf_op jit(solution)/shard_map/while/body/eval_jaxpr/jit(_take)/gather | solution.py:28
  99.0 2.2 %bitcast_convert_fusion.3 = (f32[16,2,32,1024]{3,0,1,2:T(8,128)S(1)}, f32[16,2,32,1024]{3,0,1,2:T(8,128)S(1)}) fusion(bf16[32,16,2,1024]{3,1,2,0:T(8,128)(2,1)} %gather_fusion, pred[32]{0:T(512)(128)(4,1)S(1)} %get-tuple-element.126, bf16[32,16,2,1024]{3,1,2,0:T(8,128)(2,1)S(1)} %gather_fusion.1, pred[32]{0:T(512)(128)(4,1)S(1)} %get-tuple-element.128), kind=kLoop, calls=%fused_computation.8.clone.1 | loop fusion | flops 4194304 | bytes 12582976 | tf_op jit(solution)/shard_map/while/body/eval_jaxpr/convert_element_type | solution.py:28
  101.2 2.1 %multiply_convert_fusion.5 = (bf16[16,1,32,1024]{3,0,1,2:T(8,128)(2,1)S(1)}, bf16[16,1,32,1024]{3,0,1,2:T(8,128)(2,1)}) fusion(f32[16,2,32,1024]{3,0,1,2:T(8,128)S(1)} %get-tuple-element.129, f32[16,2,32,1024]{3,0,1,2:T(8,128)S(1)} %get-tuple-element.130, f32[1024]{0:T(1024)S(1)} %get-tuple-element.153), kind=kLoop, calls=%fused_computation.12.clone.1 | loop fusion | flops 5242880 | bytes 10489856 | tf_op jit(solution)/shard_map/convert
  103.4 2.9 %gather_fusion.2 = bf16[32,16,2,1024]{3,1,2,0:T(8,128)(2,1)S(1)} fusion(bf16[16,2,64,1024]{3,0,2,1:T(8,128)(2,1)} %get-tuple-element.152, s32[1024]{0:T(1024)S(1)} %pad_clamp_fusion.8), kind=kCustom, calls=%fused_computation.clone.clone.1 | custom fusion | bytes 4194432 | tf_op jit(solution)/shard_map/while/body/eval_jaxpr/jit(_take)/gather | solution.py:29
  106.2 5.4 %fusion.27 = f32[32,16,2,16,2]{3,1,4,2,0:T(8,128)} fusion(bf16[16,1,32,1024]{3,0,1,2:T(8,128)(2,1)} %get-tuple-element.131, bf16[16,1,32,1024]{3,0,1,2:T(8,128)(2,1)S(1)} %get-tuple-element.132, bf16[32,16,2,1024]{3,1,2,0:T(8,128)(2,1)S(1)} %gather_fusion.2, pred[32]{0:T(512)(128)(4,1)S(1)} %get-tuple-element.134), kind=kOutput, calls=%fused_computation.4.clone.1 | convolution fusion | flops 72351744 | bytes 4325408 | tf_op jit(solution)/shard_map/while/body/eval_jaxpr/ictx,jdtx->tcdij/dot_general | solution.py:37
  111.6 1.9 %copy.34 = f32[32,16,2,16,2]{0,1,3,2,4:T(8,128)S(1)} copy(f32[32,16,2,16,2]{3,1,4,2,0:T(8,128)} %fusion.27) | data formatting | bytes 262144 | tf_op jit(solution)/shard_map/while/body/eval_jaxpr/ictx,jdtx->tcdij/dot_general | solution.py:37
  113.5 0.1 copy.35
  113.7 2.9 %gather_fusion.1 = bf16[32,16,2,1024]{3,1,2,0:T(8,128)(2,1)S(1)} fusion(bf16[16,2,64,1024]{3,0,2,1:T(8,128)(2,1)} %get-tuple-element.152, s32[1024]{0:T(1024)S(1)} %pad_clamp_fusion.7), kind=kCustom, calls=%fused_computation.1.clone.clone.1 | custom fusion | bytes 4194432 | tf_op jit(solution)/shard_map/while/body/eval_jaxpr/jit(_take)/gather | solution.py:27
  116.6 4.2 %gather_fusion = bf16[32,16,2,1024]{3,1,2,0:T(8,128)(2,1)} fusion(bf16[16,2,64,1024]{3,0,2,1:T(8,128)(2,1)} %get-tuple-element.152, s32[1024]{0:T(1024)S(1)} %pad_clamp_fusion.6), kind=kCustom, calls=%fused_computation.2.clone.clone.1 | custom fusion | bytes 4194432 | tf_op jit(solution)/shard_map/while/body/eval_jaxpr/jit(_take)/gather | solution.py:28
  120.8 2.2 %bitcast_convert_fusion.3 = (f32[16,2,32,1024]{3,0,1,2:T(8,128)S(1)}, f32[16,2,32,1024]{3,0,1,2:T(8,128)S(1)}) fusion(bf16[32,16,2,1024]{3,1,2,0:T(8,128)(2,1)} %gather_fusion, pred[32]{0:T(512)(128)(4,1)S(1)} %get-tuple-element.126, bf16[32,16,2,1024]{3,1,2,0:T(8,128)(2,1)S(1)} %gather_fusion.1, pred[32]{0:T(512)(128)(4,1)S(1)} %get-tuple-element.128), kind=kLoop, calls=%fused_computation.8.clone.1 | loop fusion | flops 4194304 | bytes 12582976 | tf_op jit(solution)/shard_map/while/body/eval_jaxpr/convert_element_type | solution.py:28
  123.0 2.1 %multiply_convert_fusion.5 = (bf16[16,1,32,1024]{3,0,1,2:T(8,128)(2,1)S(1)}, bf16[16,1,32,1024]{3,0,1,2:T(8,128)(2,1)}) fusion(f32[16,2,32,1024]{3,0,1,2:T(8,128)S(1)} %get-tuple-element.129, f32[16,2,32,1024]{3,0,1,2:T(8,128)S(1)} %get-tuple-element.130, f32[1024]{0:T(1024)S(1)} %get-tuple-element.153), kind=kLoop, calls=%fused_computation.12.clone.1 | loop fusion | flops 5242880 | bytes 10489856 | tf_op jit(solution)/shard_map/convert
  125.2 2.9 %gather_fusion.2 = bf16[32,16,2,1024]{3,1,2,0:T(8,128)(2,1)S(1)} fusion(bf16[16,2,64,1024]{3,0,2,1:T(8,128)(2,1)} %get-tuple-element.152, s32[1024]{0:T(1024)S(1)} %pad_clamp_fusion.8), kind=kCustom, calls=%fused_computation.clone.clone.1 | custom fusion | bytes 4194432 | tf_op jit(solution)/shard_map/while/body/eval_jaxpr/jit(_take)/gather | solution.py:29
  128.0 5.4 %fusion.27 = f32[32,16,2,16,2]{3,1,4,2,0:T(8,128)} fusion(bf16[16,1,32,1024]{3,0,1,2:T(8,128)(2,1)} %get-tuple-element.131, bf16[16,1,32,1024]{3,0,1,2:T(8,128)(2,1)S(1)} %get-tuple-element.132, bf16[32,16,2,1024]{3,1,2,0:T(8,128)(2,1)S(1)} %gather_fusion.2, pred[32]{0:T(512)(128)(4,1)S(1)} %get-tuple-element.134), kind=kOutput, calls=%fused_computation.4.clone.1 | convolution fusion | flops 72351744 | bytes 4325408 | tf_op jit(solution)/shard_map/while/body/eval_jaxpr/ictx,jdtx->tcdij/dot_general | solution.py:37
  133.4 1.9 %copy.34 = f32[32,16,2,16,2]{0,1,3,2,4:T(8,128)S(1)} copy(f32[32,16,2,16,2]{3,1,4,2,0:T(8,128)} %fusion.27) | data formatting | bytes 262144 | tf_op jit(solution)/shard_map/while/body/eval_jaxpr/ictx,jdtx->tcdij/dot_general | solution.py:37
  135.3 0.1 copy.35
  135.5 0.0 copy-start
  135.5 0.6 copy-done
  136.1 0.0 reduce-scatter.2.cloned.1.call-update
  136.1 0.0 copy-done.2
  136.1 0.6 dynamic-slice
  137.4 19.5 %reduce-scatter.2.cloned.1.call-done = f32[16,512]{1,0:T(8,128)} async-done(((f32[64,512]{1,0:T(8,128)}), f32[16,512]{1,0:T(8,128)}) %reduce-scatter.2.cloned.1.call-update) | async-done | bytes 32784 | tf_op jit(solution)/shard_map/reduce_scatter | solution.py:73
  156.8 10.8 %all-reduce = f32[16,512]{1,0:T(8,128)S(1)} all-reduce(f32[16,512]{1,0:T(8,128)} %reduce-scatter.2.cloned.1.call-done), channel_id=3, replica_groups=mesh['groups'=2,'space'=4,'freq'=2,'band'=2] {'freq','band'}, use_global_device_ids=true, to_apply=%region_3.5.clone | all-reduce | flops 8192 | bytes 65536
  167.6 0.6 constant_dynamic-slice_fusion.1
  (19 shorter events, 0.3 us)
Async XLA Ops:
  21.1 5.1 %copy-start.1 = (s32[64,2]{0,1:T(2,128)S(1)}, s32[64,2]{0,1:T(2,128)}, u32[]{:S(2)}) copy-start(s32[64,2]{0,1:T(2,128)} %param.9) | copy-start | bytes 1540
  21.1 53.9 %all-to-all-start = ((bf16[4,128,4096]{1,0,2:T(4,128)(2,1)}), bf16[4,128,4096]{1,0,2:T(4,128)(2,1)}, u32[]{:S(2)}, u32[]{:S(2)}) async-start(bf16[4,128,4096]{1,0,2:T(4,128)(2,1)} %copy.23), calls=%async_computation | async-start | bytes 8388608 | tf_op jit(solution)/shard_map/all_to_all | solution.py:68
  26.1 130.8 %reduce-scatter.2.cloned.1.call-start = ((), (), s32[]{:S(2)}) async-start(), calls=%async_computation.2 | async-start | bytes 163840 | tf_op jit(solution)/shard_map/reduce_scatter | solution.py:73
  85.0 6.9 %dynamic-slice-start = ((f32[4096]{0:T(1024)}, s32[]{:T(128)}), f32[1024]{0:T(1024)S(1)}, s32[]{:S(2)}) async-start(f32[4096]{0:T(1024)} %param.8, s32[]{:T(128)} %select_n.20), calls=%async_computation.3 | async-start | bytes 8704 | tf_op jit(solution)/shard_map/dynamic_slice | solution.py:70
  91.9 44.2 %copy-start.2 = (u32[32]{0:T(128)S(1)}, u32[32]{0:T(128)}, u32[]{:S(2)}) copy-start(u32[32]{0:T(128)} %constant.60) | copy-start | bytes 388
  135.5 0.6 copy-start
Sparse Core Ops, SparseCore 0:
  136.2 20.5 reduce-scatter.1
where the time goes:
time: 176 us; the launch traced here: 175 us
  waiting for transfers between devices  68.2 us (39%)
  local copies, waits for them, and re-layouts  50.2 us (29%)
  matrix products  17.4 us (10%)
  between operations  14.1 us (8%)
  blocking collectives  10.8 us (6%)
  other arithmetic  9.2 us (5%)
  starting transfers between devices  5.01 us (3%)
    all_to_all x1, waiting for transfers between devices, per_device(): lax.all_to_all(spec_local, ('freq', 'band'), split_axis=2, concat_axis=0,...  48.7 us
    reduce_scatter x1, waiting for transfers between devices, per_device(): lax.psum_scatter(block_terms(spectra, weights_own, triads, point_scale),...  19.5 us
    unnamed x1, blocking collectives  10.8 us
    dot_general x2, matrix products, triad_block(): jnp.einsum('ictx,jdtx->tcdij', field_a, third_spec, preferred_element_typ...  10.7 us
    all_to_all x1, local copies, waits for them, and re-layouts, per_device(): lax.all_to_all(spec_local, ('freq', 'band'), split_axis=2, concat_axis=0,...  10 us
    gather x2, local copies, waits for them, and re-layouts, triad_block(): jnp.take(spectra_grid, second_freq, axis=2).astype(jnp.float32)  8.4 us
    convert_element_type x1, local copies, waits for them, and re-layouts, per_device(): spec_local = jnp.einsum('ct,btx->bcx', dft_table, snapshots, preferred_el...  7.54 us
    reshape x1, local copies, waits for them, and re-layouts, block_terms(): spectra_grid = spectra.reshape(NB, 2, NF, columns)  6.92 us
  transfers between devices with their start and end apart: 2, of which 2 were waited for; matrix products, arithmetic and copies ran while one was open for 0% of the time, Pallas kernels for 0%

commit v1 on v0

--- a/solution.py
+++ b/solution.py
@@ -65,7 +65,16 @@
     ).astype(jnp.bfloat16)
     point_scale = 1.0 / math.sqrt(points * lax.axis_size("space"))
     shard_count = lax.axis_size("freq") * lax.axis_size("band")
-    spectra = lax.all_to_all(spec_local, ("freq", "band"), split_axis=2, concat_axis=0, tiled=True)
+
+    def post_the_quarters(z_in, peer_axis):
+        return jnp.concatenate(
+            lax.all_to_all(
+                jnp.stack(jnp.split(z_in, lax.axis_size(peer_axis), 2), 0), peer_axis, 0, 0
+            ),
+            axis=0,
+        )
+
+    spectra = post_the_quarters(spec_local, ("freq", "band"))
     own_points = points // shard_count
     weights_own = lax.dynamic_slice_in_dim(
         weights, lax.axis_index(("freq", "band")) * own_points, own_points

time: 176 us -> 159 us (0.903)
  local copies, waits for them, and re-layouts: 50.2 us -> 32.6 us
  other arithmetic: 9.2 us -> 11.4 us
  matrix products: 17.4 us -> 15.4 us
    all_to_all x1 -> x0, local copies, waits for them, and re-layouts: 10 us -> none  [per_device(): lax.all_to_all(spec_local, ('freq', 'band'), split_axis=2, concat_axis=0,...]
    convert_element_type x1 -> x0, local copies, waits for them, and re-layouts: 7.54 us -> none  [per_device(): spec_local = jnp.einsum('ct,btx->bcx', dft_table, snapshots, preferred_el...]
    reshape x1 -> x0, local copies, waits for them, and re-layouts: 6.92 us -> none  [block_terms(): spectra_grid = spectra.reshape(NB, 2, NF, columns)]
    while x0 -> x1, local copies, waits for them, and re-layouts: none -> 6.47 us  [block_terms(): result = lax.map(one_group, grouped)]
    another operation x3 -> x4, other arithmetic: 4.52 us -> 6.75 us
    dot_general x1, matrix products: 6.62 us -> 4.66 us  [per_device(): jnp.einsum('ct,btx->bcx', dft_table, snapshots, preferred_element_type=jn...]
where the time goes in v1:
time: 159 us; the launch traced here: 158 us
  waiting for transfers between devices  68.2 us (43%)
  local copies, waits for them, and re-layouts  32.6 us (21%)
  matrix products  15.4 us (10%)
  between operations  14.2 us (9%)
  other arithmetic  11.4 us (7%)
  blocking collectives  10.8 us (7%)
  starting transfers between devices  5.01 us (3%)
    all_to_all x1, waiting for transfers between devices, post_the_quarters(): lax.all_to_all(jnp.stack(jnp.split(z_in, lax.axis_size(peer_axis), 2), 0)...  48.7 us
    reduce_scatter x1, waiting for transfers between devices, per_device(): lax.psum_scatter(block_terms(spectra, weights_own, triads, point_scale),...  19.4 us
    unnamed x1, blocking collectives  10.8 us
    dot_general x2, matrix products, triad_block(): jnp.einsum('ictx,jdtx->tcdij', field_a, third_spec, preferred_element_typ...  10.7 us
    gather x2, local copies, waits for them, and re-layouts, triad_block(): jnp.take(spectra_grid, second_freq, axis=2).astype(jnp.float32)  8.39 us
    while x1, local copies, waits for them, and re-layouts, block_terms(): result = lax.map(one_group, grouped)  6.47 us
    gather x2, local copies, waits for them, and re-layouts, triad_block(): first_spec = jnp.take(spectra_grid, first_freq, axis=2).astype(jnp.float32)  5.74 us
    gather x2, local copies, waits for them, and re-layouts, triad_block(): third_spec = jnp.take(spectra_grid, third_freq, axis=2)  5.73 us
  transfers between devices with their start and end apart: 2, of which 2 were waited for; matrix products, arithmetic and copies ran while one was open for 0% of the time, Pallas kernels for 0%

profile of v1, /device:TPU:0, one launch (start us, length us, event | category | flops | bytes accessed | tf_op | source)
XLA Modules:
  0.0 157.8 jit_solution(16919528808621779772)
XLA Ops:
  6.6 0.3 multiply_convert_fusion.2
  6.9 4.7 %fusion.11 = bf16[4,128,4096]{2,1,0:T(8,128)(2,1)S(1)} fusion(bf16[4,256,4096]{2,1,0:T(8,128)(2,1)} %param.7, bf16[64,256]{1,0:T(8,128)(2,1)S(1)} %get-tuple-element.84, bf16[64,256]{1,0:T(8,128)(2,1)S(1)} %get-tuple-element.85), kind=kOutput, calls=%fused_computation.35 | convolution fusion | flops 1075970048 | bytes 12648448 | tf_op jit(solution)/shard_map/ct,btx->bcx/dot_general | solution.py:63
  11.6 0.4 slice_bitcast_fusion.3
  12.0 2.2 %pad_maximum_fusion = bf16[4,4,128,1024]{3,2,1,0:T(8,128)(2,1)} fusion(bf16[1,4,128,1024]{3,2,1,0:T(8,128)(2,1)S(1)} %get-tuple-element.81, bf16[1,4,128,1024]{3,2,1,0:T(8,128)(2,1)S(1)} %get-tuple-element.82, bf16[1,4,128,1024]{3,2,1,0:T(8,128)(2,1)S(1)} %get-tuple-element.83, bf16[1,4,128,1024]{3,2,1,0:T(8,128)(2,1)S(1)} %get-tuple-element.80), kind=kLoop, calls=%fused_computation.36 | loop fusion | flops 6291456 | bytes 8388608 | tf_op jit(solution)/shard_map/stack | solution.py:72
  14.2 0.0 copy-start.1
  14.2 5.0 %all-to-all-start = ((bf16[4,4,128,1024]{3,2,1,0:T(8,128)(2,1)}), bf16[4,4,128,1024]{3,2,1,0:T(8,128)(2,1)}, u32[]{:S(2)}, u32[]{:S(2)}) async-start(bf16[4,4,128,1024]{3,2,1,0:T(8,128)(2,1)} %pad_maximum_fusion), calls=%async_computation | async-start | bytes 8388608 | tf_op jit(solution)/shard_map/all_to_all | solution.py:71
  19.2 0.0 reduce-scatter.2.cloned.1.call-start
  19.3 0.0 copy-done.1
  19.3 0.1 reshape.73
  19.4 48.7 %all-to-all-done = bf16[4,4,128,1024]{3,2,1,0:T(8,128)(2,1)} async-done(((bf16[4,4,128,1024]{3,2,1,0:T(8,128)(2,1)}), bf16[4,4,128,1024]{3,2,1,0:T(8,128)(2,1)}, u32[]{:S(2)}, u32[]{:S(2)}) %all-to-all-start) | async-done | bytes 4194336 | tf_op jit(solution)/shard_map/all_to_all | solution.py:71
  68.1 0.0 dynamic-slice-start
  68.1 6.5 %copy.22 = bf16[16,2,64,1024]{3,0,2,1:T(8,128)(2,1)} copy(bf16[16,2,64,1024]{3,2,1,0:T(8,128)(2,1)} %bitcast.20) | data formatting | bytes 8388608 | tf_op jit(solution)/shard_map/while | solution.py:56
  74.6 0.0 dynamic-slice-done
  74.6 0.0 copy-start.2
  74.6 43.5 %while.10 = (s32[]{:T(128)}, f32[2,32,512]{2,1,0:T(8,128)S(1)}, s32[2,32,2]{1,0,2:T(2,128)S(1)}, bf16[16,2,64,1024]{3,0,2,1:T(8,128)(2,1)}, f32[1024]{0:T(1024)S(1)}, /*index=5*/s32[]{:T(128)}) while((s32[]{:T(128)}, f32[2,32,512]{2,1,0:T(8,128)S(1)}, s32[2,32,2]{1,0,2:T(2,128)S(1)}, bf16[16,2,64,1024]{3,0,2,1:T(8,128)(2,1)}, ...), condition=%wide.region_1.3_spmd, body=%wide.region_0.2_spmd.sunk | while | flops 81841760 | bytes 40847500 | solution.py:56
  74.7 2.9 %gather_fusion.1 = bf16[32,16,2,1024]{3,1,2,0:T(8,128)(2,1)S(1)} fusion(bf16[16,2,64,1024]{3,0,2,1:T(8,128)(2,1)} %get-tuple-element.156, s32[1024]{0:T(1024)S(1)} %pad_clamp_fusion.7), kind=kCustom, calls=%fused_computation.1.clone.clone.1 | custom fusion | bytes 4194432 | tf_op jit(solution)/shard_map/while/body/eval_jaxpr/jit(_take)/gather | solution.py:27
  77.5 4.2 %gather_fusion = bf16[32,16,2,1024]{3,1,2,0:T(8,128)(2,1)} fusion(bf16[16,2,64,1024]{3,0,2,1:T(8,128)(2,1)} %get-tuple-element.156, s32[1024]{0:T(1024)S(1)} %pad_clamp_fusion.6), kind=kCustom, calls=%fused_computation.2.clone.clone.1 | custom fusion | bytes 4194432 | tf_op jit(solution)/shard_map/while/body/eval_jaxpr/jit(_take)/gather | solution.py:28
  81.7 2.2 %bitcast_convert_fusion.3 = (f32[16,2,32,1024]{3,0,1,2:T(8,128)S(1)}, f32[16,2,32,1024]{3,0,1,2:T(8,128)S(1)}) fusion(bf16[32,16,2,1024]{3,1,2,0:T(8,128)(2,1)} %gather_fusion, pred[32]{0:T(512)(128)(4,1)S(1)} %get-tuple-element.130, bf16[32,16,2,1024]{3,1,2,0:T(8,128)(2,1)S(1)} %gather_fusion.1, pred[32]{0:T(512)(128)(4,1)S(1)} %get-tuple-element.132), kind=kLoop, calls=%fused_computation.8.clone.1 | loop fusion | flops 4194304 | bytes 12582976 | tf_op jit(solution)/shard_map/while/body/eval_jaxpr/convert_element_type | solution.py:28
  83.9 2.1 %multiply_convert_fusion.5 = (bf16[16,1,32,1024]{3,0,1,2:T(8,128)(2,1)S(1)}, bf16[16,1,32,1024]{3,0,1,2:T(8,128)(2,1)}) fusion(f32[16,2,32,1024]{3,0,1,2:T(8,128)S(1)} %get-tuple-element.133, f32[16,2,32,1024]{3,0,1,2:T(8,128)S(1)} %get-tuple-element.134, f32[1024]{0:T(1024)S(1)} %get-tuple-element.157), kind=kLoop, calls=%fused_computation.12.clone.1 | loop fusion | flops 5242880 | bytes 10489856 | tf_op jit(solution)/shard_map/convert
  86.1 2.9 %gather_fusion.2 = bf16[32,16,2,1024]{3,1,2,0:T(8,128)(2,1)S(1)} fusion(bf16[16,2,64,1024]{3,0,2,1:T(8,128)(2,1)} %get-tuple-element.156, s32[1024]{0:T(1024)S(1)} %pad_clamp_fusion.8), kind=kCustom, calls=%fused_computation.clone.clone.1 | custom fusion | bytes 4194432 | tf_op jit(solution)/shard_map/while/body/eval_jaxpr/jit(_take)/gather | solution.py:29
  89.0 5.4 %fusion.27 = f32[32,16,2,16,2]{3,1,4,2,0:T(8,128)} fusion(bf16[16,1,32,1024]{3,0,1,2:T(8,128)(2,1)} %get-tuple-element.135, bf16[16,1,32,1024]{3,0,1,2:T(8,128)(2,1)S(1)} %get-tuple-element.136, bf16[32,16,2,1024]{3,1,2,0:T(8,128)(2,1)S(1)} %gather_fusion.2, pred[32]{0:T(512)(128)(4,1)S(1)} %get-tuple-element.138), kind=kOutput, calls=%fused_computation.4.clone.1 | convolution fusion | flops 72351744 | bytes 4325408 | tf_op jit(solution)/shard_map/while/body/eval_jaxpr/ictx,jdtx->tcdij/dot_general | solution.py:37
  94.3 1.9 %copy.31 = f32[32,16,2,16,2]{0,1,3,2,4:T(8,128)S(1)} copy(f32[32,16,2,16,2]{3,1,4,2,0:T(8,128)} %fusion.27) | data formatting | bytes 262144 | tf_op jit(solution)/shard_map/while/body/eval_jaxpr/ictx,jdtx->tcdij/dot_general | solution.py:37
  96.2 0.1 copy.32
  96.4 2.9 %gather_fusion.1 = bf16[32,16,2,1024]{3,1,2,0:T(8,128)(2,1)S(1)} fusion(bf16[16,2,64,1024]{3,0,2,1:T(8,128)(2,1)} %get-tuple-element.156, s32[1024]{0:T(1024)S(1)} %pad_clamp_fusion.7), kind=kCustom, calls=%fused_computation.1.clone.clone.1 | custom fusion | bytes 4194432 | tf_op jit(solution)/shard_map/while/body/eval_jaxpr/jit(_take)/gather | solution.py:27
  99.3 4.2 %gather_fusion = bf16[32,16,2,1024]{3,1,2,0:T(8,128)(2,1)} fusion(bf16[16,2,64,1024]{3,0,2,1:T(8,128)(2,1)} %get-tuple-element.156, s32[1024]{0:T(1024)S(1)} %pad_clamp_fusion.6), kind=kCustom, calls=%fused_computation.2.clone.clone.1 | custom fusion | bytes 4194432 | tf_op jit(solution)/shard_map/while/body/eval_jaxpr/jit(_take)/gather | solution.py:28
  103.5 2.2 %bitcast_convert_fusion.3 = (f32[16,2,32,1024]{3,0,1,2:T(8,128)S(1)}, f32[16,2,32,1024]{3,0,1,2:T(8,128)S(1)}) fusion(bf16[32,16,2,1024]{3,1,2,0:T(8,128)(2,1)} %gather_fusion, pred[32]{0:T(512)(128)(4,1)S(1)} %get-tuple-element.130, bf16[32,16,2,1024]{3,1,2,0:T(8,128)(2,1)S(1)} %gather_fusion.1, pred[32]{0:T(512)(128)(4,1)S(1)} %get-tuple-element.132), kind=kLoop, calls=%fused_computation.8.clone.1 | loop fusion | flops 4194304 | bytes 12582976 | tf_op jit(solution)/shard_map/while/body/eval_jaxpr/convert_element_type | solution.py:28
  105.7 2.1 %multiply_convert_fusion.5 = (bf16[16,1,32,1024]{3,0,1,2:T(8,128)(2,1)S(1)}, bf16[16,1,32,1024]{3,0,1,2:T(8,128)(2,1)}) fusion(f32[16,2,32,1024]{3,0,1,2:T(8,128)S(1)} %get-tuple-element.133, f32[16,2,32,1024]{3,0,1,2:T(8,128)S(1)} %get-tuple-element.134, f32[1024]{0:T(1024)S(1)} %get-tuple-element.157), kind=kLoop, calls=%fused_computation.12.clone.1 | loop fusion | flops 5242880 | bytes 10489856 | tf_op jit(solution)/shard_map/convert
  107.9 2.9 %gather_fusion.2 = bf16[32,16,2,1024]{3,1,2,0:T(8,128)(2,1)S(1)} fusion(bf16[16,2,64,1024]{3,0,2,1:T(8,128)(2,1)} %get-tuple-element.156, s32[1024]{0:T(1024)S(1)} %pad_clamp_fusion.8), kind=kCustom, calls=%fused_computation.clone.clone.1 | custom fusion | bytes 4194432 | tf_op jit(solution)/shard_map/while/body/eval_jaxpr/jit(_take)/gather | solution.py:29
  110.7 5.4 %fusion.27 = f32[32,16,2,16,2]{3,1,4,2,0:T(8,128)} fusion(bf16[16,1,32,1024]{3,0,1,2:T(8,128)(2,1)} %get-tuple-element.135, bf16[16,1,32,1024]{3,0,1,2:T(8,128)(2,1)S(1)} %get-tuple-element.136, bf16[32,16,2,1024]{3,1,2,0:T(8,128)(2,1)S(1)} %gather_fusion.2, pred[32]{0:T(512)(128)(4,1)S(1)} %get-tuple-element.138), kind=kOutput, calls=%fused_computation.4.clone.1 | convolution fusion | flops 72351744 | bytes 4325408 | tf_op jit(solution)/shard_map/while/body/eval_jaxpr/ictx,jdtx->tcdij/dot_general | solution.py:37
  116.1 1.9 %copy.31 = f32[32,16,2,16,2]{0,1,3,2,4:T(8,128)S(1)} copy(f32[32,16,2,16,2]{3,1,4,2,0:T(8,128)} %fusion.27) | data formatting | bytes 262144 | tf_op jit(solution)/shard_map/while/body/eval_jaxpr/ictx,jdtx->tcdij/dot_general | solution.py:37
  118.0 0.1 copy.32
  118.2 0.0 copy-start
  118.2 0.6 copy-done
  118.8 0.0 reduce-scatter.2.cloned.1.call-update
  118.8 0.0 copy-done.2
  118.8 0.6 dynamic-slice
  120.1 19.4 %reduce-scatter.2.cloned.1.call-done = f32[16,512]{1,0:T(8,128)} async-done(((f32[64,512]{1,0:T(8,128)}), f32[16,512]{1,0:T(8,128)}) %reduce-scatter.2.cloned.1.call-update) | async-done | bytes 32784 | tf_op jit(solution)/shard_map/reduce_scatter | solution.py:82
  139.5 10.8 %all-reduce = f32[16,512]{1,0:T(8,128)S(1)} all-reduce(f32[16,512]{1,0:T(8,128)} %reduce-scatter.2.cloned.1.call-done), channel_id=3, replica_groups=mesh['groups'=2,'space'=4,'freq'=2,'band'=2] {'freq','band'}, use_global_device_ids=true, to_apply=%region_3.5.clone | all-reduce | flops 8192 | bytes 65536
  150.3 0.6 constant_dynamic-slice_fusion.1
  (19 shorter events, 0.3 us)
Async XLA Ops:
  14.2 5.1 %copy-start.1 = (s32[64,2]{0,1:T(2,128)S(1)}, s32[64,2]{0,1:T(2,128)}, u32[]{:S(2)}) copy-start(s32[64,2]{0,1:T(2,128)} %param.9) | copy-start | bytes 1540
  14.2 53.9 %all-to-all-start = ((bf16[4,4,128,1024]{3,2,1,0:T(8,128)(2,1)}), bf16[4,4,128,1024]{3,2,1,0:T(8,128)(2,1)}, u32[]{:S(2)}, u32[]{:S(2)}) async-start(bf16[4,4,128,1024]{3,2,1,0:T(8,128)(2,1)} %pad_maximum_fusion), calls=%async_computation | async-start | bytes 8388608 | tf_op jit(solution)/shard_map/all_to_all | solution.py:71
  19.2 120.3 %reduce-scatter.2.cloned.1.call-start = ((), (), s32[]{:S(2)}) async-start(), calls=%async_computation.2 | async-start | bytes 163840 | tf_op jit(solution)/shard_map/reduce_scatter | solution.py:82
  68.1 6.5 %dynamic-slice-start = ((f32[4096]{0:T(1024)}, s32[]{:T(128)}), f32[1024]{0:T(1024)S(1)}, s32[]{:S(2)}) async-start(f32[4096]{0:T(1024)} %param.8, s32[]{:T(128)} %select_n.20), calls=%async_computation.3 | async-start | bytes 8704 | tf_op jit(solution)/shard_map/dynamic_slice | solution.py:79
  74.6 44.2 %copy-start.2 = (u32[32]{0:T(128)S(1)}, u32[32]{0:T(128)}, u32[]{:S(2)}) copy-start(u32[32]{0:T(128)} %constant.60) | copy-start | bytes 388
  118.2 0.6 copy-start
Sparse Core Ops, SparseCore 0:
  118.9 20.5 reduce-scatter.1
